TPU v7x, 256 devices: a whole 4x4x8 slice. The times are simulated.
256 devices in a mesh: slab: 32 (over z, y), snap: 8 (over x, core).
Axes of the slice: x: 4, y: 4, z: 8, core: 2. Of those that a mesh axis runs over, the one named last changes fastest.
Arguments:
- flow: bfloat16 [128, 3, 64, 64, 128], P('snap', None, 'slab'), may hold values from -127 to 127
- large_scale: bfloat16 [3, 64, 64, 128], P(None, 'slab'), may hold values from -6 to 6
- modulation: float32 [128, 64], replicated, may hold values from -15 to 15
- metric: float32 [4, 64, 64, 128], P(None, 'slab'), may hold values from -0.5 to 9.6
Outputs:
- whitened: float32 [128, 3, 64, 64, 128], P(None, None, 'slab', 'snap')
All inputs are finite; a program needn't handle non-finite values.
Results may differ from a plain program's by a relative error of at most 0.0003.
Values may be sent and summed in bfloat16 or wider, within the bound.
A program may use at most 64 MiB of HBM per device.

v0:
```python
import jax
import jax.numpy as jnp
from jax import lax
from jax.sharding import PartitionSpec as P

NSITER = 6


def with_halo(block, sides, width):
    for axis, dim in sides:
        count = lax.axis_size(axis)
        forward = [(i, i + 1) for i in range(count - 1)]
        backward = [(target, source) for source, target in forward]
        low = lax.ppermute(
            lax.slice_in_dim(block, block.shape[dim] - width, None, axis=dim), axis, forward
        )
        high = lax.ppermute(lax.slice_in_dim(block, 0, width, axis=dim), axis, backward)
        block = jnp.concatenate([low, block, high], axis=dim)
    return block


def vorticity(velocity, metric):
    metric_x = metric[0]
    shear_xy = metric[1]
    metric_y = metric[2]
    metric_z = metric[3]

    def along_x(values):
        return 0.5 * (values[..., 1:-1, 2:, :] - values[..., 1:-1, :-2, :])

    def along_y(values):
        return 0.5 * (values[..., 2:, 1:-1, :] - values[..., :-2, 1:-1, :])

    def along_z(values):
        center = values[..., 1:-1, 1:-1, :]
        return 0.5 * (jnp.roll(center, -1, -1) - jnp.roll(center, 1, -1))

    def slope_x(values):
        return metric_x * along_x(values) + shear_xy * along_y(values)

    def slope_y(values):
        return metric_y * along_y(values)

    def slope_z(values):
        return metric_z * along_z(values)

    stream = velocity[..., 0, :, :, :]
    normal = velocity[..., 1, :, :, :]
    spanwise = velocity[..., 2, :, :, :]
    around_x = slope_y(spanwise) - slope_z(normal)
    around_y = slope_z(stream) - slope_x(spanwise)
    around_z = slope_x(normal) - slope_y(stream)
    return jnp.stack([around_x, around_y, around_z], axis=-4)


def wrap_columns(values):
    return jnp.concatenate([values[..., -1:, :], values, values[..., :1, :]], axis=-2)


def whitening(correlation):
    identity = jnp.eye(correlation.shape[0], dtype=correlation.dtype)
    frob_scale = jnp.sqrt(jnp.sum(correlation * correlation) + 1e-06)
    approx = correlation / frob_scale
    inverse = identity
    for repeat in range(NSITER):
        factor = 0.5 * (3.0 * identity - jnp.dot(inverse, approx, precision=lax.Precision.HIGHEST))
        approx = jnp.dot(approx, factor, precision=lax.Precision.HIGHEST)
        inverse = jnp.dot(factor, inverse, precision=lax.Precision.HIGHEST)
    return inverse / jnp.sqrt(frob_scale)


def inner_rows(left_rows, right_rows):
    return lax.dot_general(
        left_rows,
        right_rows,
        (((1,), (1,)), ((), ())),
        precision=lax.Precision.HIGHEST,
        preferred_element_type=jnp.float32,
    )


def planes_padded(flow, large_scale):
    joined = jnp.concatenate([flow, large_scale[None]], axis=0)
    return with_halo(joined, (("slab", 2),), 1)


def per_device(flow, large_scale, modulation, metric):
    snap_count = lax.axis_size("snap")
    slab_count = lax.axis_size("slab")
    own_snaps = flow.shape[0]
    block_cols = flow.shape[3] // snap_count
    snap_index = lax.axis_index("snap")
    mod_ext = jnp.concatenate([modulation[:, -1:], modulation, modulation[:, :1]], axis=1)
    padded = planes_padded(flow, large_scale)
    large_ext = wrap_columns(padded[own_snaps].astype(jnp.float32))
    mod_mine = lax.dynamic_slice_in_dim(mod_ext, snap_index * own_snaps, own_snaps, 0)
    velocity = (
        wrap_columns(padded[:own_snaps].astype(jnp.float32))
        + mod_mine[:, None, None, :, None] * large_ext[None]
    )
    local_fields = vorticity(velocity, metric)
    pieces = local_fields.reshape(
        own_snaps, 3, local_fields.shape[2], snap_count, block_cols, local_fields.shape[4]
    )
    fields = lax.all_to_all(pieces, "snap", split_axis=3, concat_axis=0, tiled=True)[:, :, :, 0]
    snapshot_rows = fields.reshape(fields.shape[0], -1)
    gram_local = inner_rows(snapshot_rows, snapshot_rows)
    gram_total = lax.psum(gram_local, ("slab", "snap"))
    correlation = gram_total / (snapshot_rows.shape[1] * slab_count * snap_count)
    weights = whitening(correlation)
    result = jnp.dot(weights, snapshot_rows, precision=lax.Precision.HIGHEST)
    return result.reshape(fields.shape)


def solution(mesh):
    return jax.shard_map(
        per_device,
        mesh=mesh,
        in_specs=(
            P("snap", None, "slab", None, None),
            P(None, "slab", None, None),
            P(),
            P(None, "slab", None, None),
        ),
        out_specs=P(None, None, "slab", "snap", None),
        check_vma=False,
    )
```

profile of v0, /device:TPU:1, one launch (start us, length us, event | category | flops | bytes accessed | tf_op | source)
XLA Modules:
  0.0 358.1 jit_solution(2387422955889473556)
XLA Ops:
  6.5 0.0 all-reduce.2.cloned.1.call-start
  6.5 2.9 fusion.21
  9.4 4.1 %collective-permute-start = (bf16[17,3,1,64,128]{4,3,2,1,0:T(8,128)(2,1)}, bf16[17,3,1,64,128]{4,3,2,1,0:T(8,128)(2,1)S(1)}, u32[]{:S(2)}, u32[]{:S(2)}) collective-permute-start(bf16[17,3,1,64,128]{4,3,2,1,0:T(8,128)(2,1)} %get-tuple-element.20), channel_id=1, source_target_pairs={{0,8},{8,16},{16,24},{24,32},{32,40},{40,48},{48,56},{56,64},{64,7... | collective-permute-start | bytes 2506760 | tf_op jit(solution)/shard_map/ppermute | solution.py:14
  13.5 1.3 collective-permute-start.1
  14.8 0.0 copy-done.3
  14.8 0.1 dynamic-slice_maximum_fusion
  14.9 0.1 copy.10
  15.0 1.0 multiply_bitcast_fusion.2
  15.9 15.1 %collective-permute-done = bf16[17,3,1,64,128]{4,3,2,1,0:T(8,128)(2,1)S(1)} collective-permute-done((bf16[17,3,1,64,128]{4,3,2,1,0:T(8,128)(2,1)}, bf16[17,3,1,64,128]{4,3,2,1,0:T(8,128)(2,1)S(1)}, u32[]{:S(2)}, u32[]{:S(2)}) %collective-permute-start) | collective-permute-done | bytes 835616 | tf_op jit(solution)/shard_map/ppermute | solution.py:14
  31.0 3.8 %collective-permute-done.1 = bf16[17,3,1,64,128]{4,3,2,1,0:T(8,128)(2,1)S(1)} collective-permute-done((bf16[17,3,1,64,128]{4,3,2,1,0:T(8,128)(2,1)}, bf16[17,3,1,64,128]{4,3,2,1,0:T(8,128)(2,1)S(1)}, u32[]{:S(2)}, u32[]{:S(2)}) %collective-permute-start.1) | collective-permute-done | bytes 835616 | tf_op jit(solution)/shard_map/ppermute | solution.py:17
  34.8 0.0 copy-done
  34.8 0.5 pad_maximum_fusion
  35.3 0.7 slice_convert_fusion
  36.1 0.1 fusion.27
  36.3 1.5 maximum_add_fusion
  37.7 0.5 slice_bitcast_fusion.2
  38.2 0.9 fusion.28
  39.1 0.9 fusion.29
  40.0 0.8 fusion.9
  40.7 1.5 fusion.19
  42.2 0.2 pad_maximum_fusion.1
  42.5 0.3 copy.19
  42.8 43.4 %all_to_all.15 = f32[16,3,2,8,8,128]{5,4,2,1,0,3:T(8,128)} all-to-all(f32[16,3,2,8,8,128]{5,4,2,1,0,3:T(8,128)S(1)} %copy.19), channel_id=1, replica_groups=mesh['slab'=32,'snap'=8] {'snap'}, dimensions={3} | all-to-all | bytes 6291456 | tf_op jit(solution)/shard_map/all_to_all | solution.py:105
  86.2 2.8 reshape_squeeze.3
  89.0 3.2 fusion.34
  92.2 0.0 all-reduce.2.cloned.1.call-update
  92.2 2.4 copy.16
  94.6 242.7 %all-reduce.2.cloned.1.call-done = f32[128,128]{1,0:T(8,128)} async-done(((f32[128,128]{1,0:T(8,128)}), f32[128,128]{1,0:T(8,128)}) %all-reduce.2.cloned.1.call-update) | async-done | bytes 65552 | tf_op jit(solution)/shard_map/psum | solution.py:108
  337.3 1.5 multiply_reduce_fusion
  339.5 1.0 fusion.6
  340.5 0.2 fusion.23
  340.7 1.0 fusion.24
  341.8 0.2 fusion.5
  342.0 0.2 fusion.36
  342.2 0.2 fusion.35
  342.4 0.2 fusion.4
  342.6 0.2 fusion.38
  342.8 0.2 fusion.37
  343.0 0.2 fusion.3
  343.3 0.2 fusion.40
  343.5 0.2 fusion.39
  343.7 0.2 fusion.2
  343.9 0.2 fusion.41
  344.1 0.2 fusion.42
  344.3 0.2 fusion.1
  344.5 0.2 fusion
  344.7 3.0 fusion.43
  347.8 3.5 copy.17
  (10 shorter events, 0.1 us)
Async XLA Ops:
  6.5 28.2 %copy-start = (bf16[16,3,2,64,128]{4,3,2,1,0:T(8,128)(2,1)S(1)}, bf16[16,3,2,64,128]{4,3,2,1,0:T(8,128)(2,1)}, u32[]{:S(2)}) copy-start(bf16[16,3,2,64,128]{4,3,2,1,0:T(8,128)(2,1)} %param.4) | copy-start | bytes 4718596
  6.5 28.2 %copy-start.2 = (bf16[3,2,64,128]{3,2,1,0:T(8,128)(2,1)S(1)}, bf16[3,2,64,128]{3,2,1,0:T(8,128)(2,1)}, u32[]{:S(2)}) copy-start(bf16[3,2,64,128]{3,2,1,0:T(8,128)(2,1)} %param.5) | copy-start | bytes 294916
  6.5 8.2 %copy-start.3 = (f32[128,64]{0,1:T(8,128)S(1)}, f32[128,64]{0,1:T(8,128)}, u32[]{:S(2)}) copy-start(f32[128,64]{0,1:T(8,128)} %param.6) | copy-start | bytes 98308
  6.5 330.8 %all-reduce.2.cloned.1.call-start = ((), (), s32[]{:S(2)}) async-start(), calls=%async_computation.1 | async-start | bytes 131072 | tf_op jit(solution)/shard_map/psum | solution.py:108
  9.4 21.6 %collective-permute-start = (bf16[17,3,1,64,128]{4,3,2,1,0:T(8,128)(2,1)}, bf16[17,3,1,64,128]{4,3,2,1,0:T(8,128)(2,1)S(1)}, u32[]{:S(2)}, u32[]{:S(2)}) collective-permute-start(bf16[17,3,1,64,128]{4,3,2,1,0:T(8,128)(2,1)} %get-tuple-element.20), channel_id=1, source_target_pairs={{0,8},{8,16},{16,24},{24,32},{32,40},{40,48},{48,56},{56,64},{64,7... | collective-permute-start | bytes 2506760 | tf_op jit(solution)/shard_map/ppermute | solution.py:14
  13.5 21.3 %collective-permute-start.1 = (bf16[17,3,1,64,128]{4,3,2,1,0:T(8,128)(2,1)}, bf16[17,3,1,64,128]{4,3,2,1,0:T(8,128)(2,1)S(1)}, u32[]{:S(2)}, u32[]{:S(2)}) collective-permute-start(bf16[17,3,1,64,128]{4,3,2,1,0:T(8,128)(2,1)} %get-tuple-element.21), channel_id=1, source_target_pairs={{8,0},{16,8},{24,16},{32,24},{40,32},{48,40},{56,48},{64,56},{72,6... | collective-permute-start | bytes 2506760 | tf_op jit(solution)/shard_map/ppermute | solution.py:17
  94.6 250.2 %copy-start.1 = (f32[6144,128]{1,0:T(8,128)S(1)}, f32[6144,128]{1,0:T(8,128)}, u32[]{:S(2)}) copy-start(f32[6144,128]{1,0:T(8,128)} %copy.16) | copy-start | bytes 9437188
Sparse Core Ops, SparseCore 0:
  92.3 244.9 all-reduce.1
where the time goes:
time: 358 us
  waiting for transfers between devices  262 us (73%)
  blocking collectives  43.4 us (12%)
  between operations  14.4 us (4%)
  local copies, waits for them, and re-layouts  11.3 us (3%)
  matrix products  11.3 us (3%)
  other arithmetic  10.6 us (3%)
  starting transfers between devices  5.35 us (1%)
    psum x1, waiting for transfers between devices, per_device(): gram_total = lax.psum(gram_local, ('slab', 'snap'))  243 us
    all_to_all x1, blocking collectives, per_device(): lax.all_to_all(pieces, 'snap', split_axis=3, concat_axis=0, tiled=True)  43.4 us
    ppermute x1, waiting for transfers between devices, with_halo(): lax.ppermute(lax.slice_in_dim(block, block.shape[dim] - width, None, axis...  15.1 us
  transfers between devices with their start and end apart: 3, of which 3 were waited for; matrix products, arithmetic and copies ran while one was open for 1% of the time, Pallas kernels for 0%

commit v1 on v0

--- a/solution.py
+++ b/solution.py
@@ -105,7 +105,7 @@
     fields = lax.all_to_all(pieces, "snap", split_axis=3, concat_axis=0, tiled=True)[:, :, :, 0]
     snapshot_rows = fields.reshape(fields.shape[0], -1)
     gram_local = inner_rows(snapshot_rows, snapshot_rows)
-    gram_total = lax.psum(gram_local, ("slab", "snap"))
+    gram_total = lax.psum(lax.psum(gram_local, "snap"), "slab")
     correlation = gram_total / (snapshot_rows.shape[1] * slab_count * snap_count)
     weights = whitening(correlation)
     result = jnp.dot(weights, snapshot_rows, precision=lax.Precision.HIGHEST)

time: 358 us -> 325 us (0.908); the launches traced: 358 us -> 321 us
  waiting for transfers between devices: 262 us -> 224 us
    psum x1 -> x2, waiting for transfers between devices: 243 us -> 205 us  [per_device(): gram_total = lax.psum(lax.psum(gram_local, 'snap'), 'slab')]
  transfers between devices with their start and end apart: 3 -> 4, of which waited for: 3 -> 4; matrix products, arithmetic and copies ran while one was open for 1% -> 1% of each run, Pallas kernels for 0% -> 0%
where the time goes in v1:
time: 325 us; the launch traced here: 321 us
  waiting for transfers between devices  224 us (69%)
  blocking collectives  43.4 us (13%)
  between operations  14.4 us (4%)
  local copies, waits for them, and re-layouts  11.3 us (3%)
  matrix products  11.3 us (3%)
  other arithmetic  10.6 us (3%)
  starting transfers between devices  5.58 us (2%)
    psum x2, waiting for transfers between devices, per_device(): gram_total = lax.psum(lax.psum(gram_local, 'snap'), 'slab')  205 us
    all_to_all x1, blocking collectives, per_device(): lax.all_to_all(pieces, 'snap', split_axis=3, concat_axis=0, tiled=True)  43.4 us
    ppermute x1, waiting for transfers between devices, with_halo(): lax.ppermute(lax.slice_in_dim(block, block.shape[dim] - width, None, axis...  15.1 us
  transfers between devices with their start and end apart: 4, of which 4 were waited for; matrix products, arithmetic and copies ran while one was open for 1% of the time, Pallas kernels for 0%

profile of v1, /device:TPU:1, one launch (start us, length us, event | category | flops | bytes accessed | tf_op | source)
XLA Modules:
  0.0 320.7 jit_solution(1808722653167383652)
XLA Ops:
  6.5 2.9 fusion.21
  9.4 4.1 %collective-permute-start = (bf16[17,3,1,64,128]{4,3,2,1,0:T(8,128)(2,1)}, bf16[17,3,1,64,128]{4,3,2,1,0:T(8,128)(2,1)S(1)}, u32[]{:S(2)}, u32[]{:S(2)}) collective-permute-start(bf16[17,3,1,64,128]{4,3,2,1,0:T(8,128)(2,1)} %get-tuple-element.20), channel_id=1, source_target_pairs={{0,8},{8,16},{16,24},{24,32},{32,40},{40,48},{48,56},{56,64},{64,7... | collective-permute-start | bytes 2506760 | tf_op jit(solution)/shard_map/ppermute | solution.py:14
  13.5 1.3 collective-permute-start.1
  14.8 0.1 dynamic-slice_maximum_fusion
  14.9 0.1 copy.10
  15.0 1.0 multiply_bitcast_fusion.2
  15.9 15.1 %collective-permute-done = bf16[17,3,1,64,128]{4,3,2,1,0:T(8,128)(2,1)S(1)} collective-permute-done((bf16[17,3,1,64,128]{4,3,2,1,0:T(8,128)(2,1)}, bf16[17,3,1,64,128]{4,3,2,1,0:T(8,128)(2,1)S(1)}, u32[]{:S(2)}, u32[]{:S(2)}) %collective-permute-start) | collective-permute-done | bytes 835616 | tf_op jit(solution)/shard_map/ppermute | solution.py:14
  31.0 3.8 %collective-permute-done.1 = bf16[17,3,1,64,128]{4,3,2,1,0:T(8,128)(2,1)S(1)} collective-permute-done((bf16[17,3,1,64,128]{4,3,2,1,0:T(8,128)(2,1)}, bf16[17,3,1,64,128]{4,3,2,1,0:T(8,128)(2,1)S(1)}, u32[]{:S(2)}, u32[]{:S(2)}) %collective-permute-start.1) | collective-permute-done | bytes 835616 | tf_op jit(solution)/shard_map/ppermute | solution.py:17
  34.8 0.5 pad_maximum_fusion
  35.3 0.7 slice_convert_fusion
  36.1 0.1 fusion.27
  36.3 1.5 maximum_add_fusion
  37.7 0.5 slice_bitcast_fusion.2
  38.2 0.9 fusion.28
  39.1 0.9 fusion.29
  40.0 0.8 fusion.9
  40.7 1.5 fusion.19
  42.2 0.2 pad_maximum_fusion.1
  42.5 0.3 copy.19
  42.8 43.4 %all_to_all.15 = f32[16,3,2,8,8,128]{5,4,2,1,0,3:T(8,128)} all-to-all(f32[16,3,2,8,8,128]{5,4,2,1,0,3:T(8,128)S(1)} %copy.19), channel_id=1, replica_groups=mesh['slab'=32,'snap'=8] {'snap'}, dimensions={3} | all-to-all | bytes 6291456 | tf_op jit(solution)/shard_map/all_to_all | solution.py:105
  86.2 2.8 reshape_squeeze.3
  89.0 3.2 %fusion.34 = f32[128,128]{1,0:T(8,128)} fusion(f32[128,6144]{1,0:T(8,128)S(1)} %reshape_squeeze.3), kind=kOutput, calls=%fused_computation.69 | convolution fusion | flops 1207959552 | bytes 3211264 | tf_op jit(solution)/shard_map/dot_general | solution.py:73
  92.2 0.0 all-reduce.3.cloned.1.call-update
  92.2 0.2 all-reduce.5.cloned.1.call-start
  92.4 65.9 %all-reduce.3.cloned.1.call-done = f32[128,128]{1,0:T(8,128)} async-done(((f32[128,128]{1,0:T(8,128)}), f32[128,128]{1,0:T(8,128)}) %all-reduce.3.cloned.1.call-update) | async-done | bytes 65552 | tf_op jit(solution)/shard_map/psum | solution.py:108
  158.4 0.0 all-reduce.5.cloned.1.call-update
  158.4 2.4 copy.16
  160.7 139.2 %all-reduce.5.cloned.1.call-done = f32[128,128]{1,0:T(8,128)} async-done(((f32[128,128]{1,0:T(8,128)}), f32[128,128]{1,0:T(8,128)}) %all-reduce.5.cloned.1.call-update) | async-done | bytes 65552 | tf_op jit(solution)/shard_map/psum | solution.py:108
  299.9 1.5 multiply_reduce_fusion
  302.1 1.0 fusion.6
  303.1 0.2 fusion.23
  303.3 1.0 fusion.24
  304.4 0.2 fusion.5
  304.6 0.2 fusion.36
  304.8 0.2 fusion.35
  305.0 0.2 fusion.4
  305.2 0.2 fusion.38
  305.4 0.2 fusion.37
  305.6 0.2 fusion.3
  305.9 0.2 fusion.40
  306.1 0.2 fusion.39
  306.3 0.2 fusion.2
  306.5 0.2 fusion.41
  306.7 0.2 fusion.42
  306.9 0.2 fusion.1
  307.1 0.2 fusion
  307.4 3.0 fusion.43
  310.4 3.5 %copy.17 = f32[128,3,2,8,128]{4,3,2,1,0:T(8,128)} copy(f32[128,3,2,8,128]{4,0,3,2,1:T(8,128)S(1)} %fusion.43) | data formatting | bytes 6291456 | tf_op jit(solution)/shard_map/dot_general | solution.py:111
  (13 shorter events, 0.1 us)
Async XLA Ops:
  6.5 28.2 %copy-start = (bf16[16,3,2,64,128]{4,3,2,1,0:T(8,128)(2,1)S(1)}, bf16[16,3,2,64,128]{4,3,2,1,0:T(8,128)(2,1)}, u32[]{:S(2)}) copy-start(bf16[16,3,2,64,128]{4,3,2,1,0:T(8,128)(2,1)} %param.4) | copy-start | bytes 4718596
  6.5 28.2 %copy-start.2 = (bf16[3,2,64,128]{3,2,1,0:T(8,128)(2,1)S(1)}, bf16[3,2,64,128]{3,2,1,0:T(8,128)(2,1)}, u32[]{:S(2)}) copy-start(bf16[3,2,64,128]{3,2,1,0:T(8,128)(2,1)} %param.5) | copy-start | bytes 294916
  6.5 8.2 %copy-start.3 = (f32[128,64]{0,1:T(8,128)S(1)}, f32[128,64]{0,1:T(8,128)}, u32[]{:S(2)}) copy-start(f32[128,64]{0,1:T(8,128)} %param.6) | copy-start | bytes 98308
  6.5 151.8 %all-reduce.3.cloned.1.call-start = ((), (), s32[]{:S(2)}) async-start(), calls=%async_computation.1 | async-start | bytes 131072 | tf_op jit(solution)/shard_map/psum | solution.py:108
  9.4 21.6 %collective-permute-start = (bf16[17,3,1,64,128]{4,3,2,1,0:T(8,128)(2,1)}, bf16[17,3,1,64,128]{4,3,2,1,0:T(8,128)(2,1)S(1)}, u32[]{:S(2)}, u32[]{:S(2)}) collective-permute-start(bf16[17,3,1,64,128]{4,3,2,1,0:T(8,128)(2,1)} %get-tuple-element.20), channel_id=1, source_target_pairs={{0,8},{8,16},{16,24},{24,32},{32,40},{40,48},{48,56},{56,64},{64,7... | collective-permute-start | bytes 2506760 | tf_op jit(solution)/shard_map/ppermute | solution.py:14
  13.5 21.3 %collective-permute-start.1 = (bf16[17,3,1,64,128]{4,3,2,1,0:T(8,128)(2,1)}, bf16[17,3,1,64,128]{4,3,2,1,0:T(8,128)(2,1)S(1)}, u32[]{:S(2)}, u32[]{:S(2)}) collective-permute-start(bf16[17,3,1,64,128]{4,3,2,1,0:T(8,128)(2,1)} %get-tuple-element.21), channel_id=1, source_target_pairs={{8,0},{16,8},{24,16},{32,24},{40,32},{48,40},{56,48},{64,56},{72,6... | collective-permute-start | bytes 2506760 | tf_op jit(solution)/shard_map/ppermute | solution.py:17
  92.2 207.7 %all-reduce.5.cloned.1.call-start = ((), (), s32[]{:S(2)}) async-start(), calls=%async_computation.2 | async-start | bytes 131072 | tf_op jit(solution)/shard_map/psum | solution.py:108
  160.7 146.6 %copy-start.1 = (f32[6144,128]{1,0:T(8,128)S(1)}, f32[6144,128]{1,0:T(8,128)}, u32[]{:S(2)}) copy-start(f32[6144,128]{1,0:T(8,128)} %copy.16) | copy-start | bytes 9437188
Sparse Core Ops, SparseCore 0:
  92.3 65.9 all-reduce.2
  161.8 138.0 all-reduce.4
